TPU v7x, 32 devices: a whole 2x2x4 slice. The times are simulated.
32 devices in a mesh: ray: 4 (over x, core), vox: 8 (over z, y).
Axes of the slice: x: 2, y: 2, z: 4, core: 2. Of those that a mesh axis runs over, the one named last changes fastest.
Arguments:
- tiles: float32 [2048, 128, 128], P(('ray', 'vox')), may hold values from -0.25 to 0.25
- tile_ray: int32 [2048], P(('ray', 'vox')), may hold values from 0 to 15
- tile_vox: int32 [2048], P(('ray', 'vox')), may hold values from 0 to 511, as said below
- tile_count: int32 [32], P(('ray', 'vox')), may hold values from 1 to 64, as said below
- travel: float32 [512, 128], P(('ray', 'vox')), may hold values from -6 to 6
Outputs:
- solution: float32 [512, 128], P('vox')
- direction: float32 [512, 128], P('vox')
Inputs may be any that keep to these rules, and one draw needn't show every extreme that they name: `tile_count`: each entry is 1 to 64; some device has exactly 64 live slots. Among the 64 slots of one device (live or not), at most 16 have voxel blocks in the same range of 64 blocks (same tile_vox // 64); on every device some range is named by exactly 16 slots.
All inputs are finite; a program needn't handle non-finite values.
Results may differ from a plain program's by a relative error of at most 0.00017.
Values sent between devices are 32-bit elements; how exact they have to be, the bound alone decides.
No kernel may reach another device: no remote copies, remote signals or barrier semaphores. Data moves between devices by JAX's collectives and lax.ppermute only.
A program may use at most 64 MiB of HBM per device.

v0:
```python
import jax
import jax.numpy as jnp
from jax import lax
from jax.sharding import PartitionSpec as P

VBD = 64
ITERS = 2
HIGH = lax.Precision.HIGHEST


def on_device(tiles, tile_ray, tile_vox, tile_count, travel):
    n_vox = lax.axis_size("vox")
    blocks_all = VBD * n_vox
    tile_num = tiles.shape[0]
    ray_blocks = travel.shape[0]
    width = travel.shape[1]
    live = (jnp.arange(tile_num, dtype=jnp.int32) < tile_count[0]).astype(jnp.float32)[:, None]
    selector = (tile_ray[None, :] == jnp.arange(ray_blocks, dtype=jnp.int32)[:, None]).astype(
        jnp.float32
    )

    def backward(ray_vec):
        rows_in = jnp.dot(selector.T, ray_vec, precision=HIGH)
        prod = jnp.einsum("tij,ti->tj", tiles, rows_in, precision=HIGH) * live
        partial_sum = jnp.zeros((blocks_all, width), jnp.float32).at[tile_vox].add(prod)
        owned = lax.psum_scatter(partial_sum, "vox", scatter_dimension=0, tiled=True)
        return lax.psum(owned, "ray")

    def ray_length(ray_vec):
        return jnp.sqrt(lax.psum(jnp.sum(ray_vec * ray_vec), ("ray", "vox")))

    def vox_length(vox_vec):
        return jnp.sqrt(lax.psum(jnp.sum(vox_vec * vox_vec), "vox"))

    beta_now = ray_length(travel)
    ray_vec = travel / beta_now
    vox_vec = backward(ray_vec)
    alpha_now = vox_length(vox_vec)
    vox_vec = vox_vec / alpha_now
    direction = vox_vec
    solution = jnp.zeros_like(vox_vec)
    phibar = beta_now
    rhobar = alpha_now
    for step in range(ITERS):
        whole = lax.all_gather(vox_vec, "vox", axis=0, tiled=True)
        forward_prod = jnp.einsum("tij,tj->ti", tiles, whole[tile_vox], precision=HIGH) * live
        ray_vec = jnp.dot(selector, forward_prod, precision=HIGH) - alpha_now * ray_vec
        beta_now = ray_length(ray_vec)
        ray_vec = ray_vec / beta_now
        vox_vec = backward(ray_vec) - beta_now * vox_vec
        alpha_now = vox_length(vox_vec)
        vox_vec = vox_vec / alpha_now
        rho_val = jnp.sqrt(rhobar * rhobar + beta_now * beta_now)
        cosine = rhobar / rho_val
        sine_val = beta_now / rho_val
        theta_val = sine_val * alpha_now
        rhobar = -cosine * alpha_now
        phi_val = cosine * phibar
        phibar = sine_val * phibar
        solution = solution + phi_val / rho_val * direction
        direction = vox_vec - theta_val / rho_val * direction
    return (solution, direction)


def solution(mesh):
    return jax.shard_map(
        on_device,
        mesh=mesh,
        in_specs=(
            P(("ray", "vox"), None, None),
            P(("ray", "vox")),
            P(("ray", "vox")),
            P(("ray", "vox")),
            P(("ray", "vox"), None),
        ),
        out_specs=(P("vox", None), P("vox", None)),
        check_vma=False,
    )
```

profile of v0, /device:TPU:0, one launch (start us, length us, event | category | flops | bytes accessed | tf_op | source)
XLA Modules:
  0.0 524.3 jit_solution(6376675607895804721)
XLA Ops:
  7.2 0.0 reduce-scatter.4.cloned.1.call-start
  7.2 1.3 multiply_reduce_fusion.5
  8.5 42.2 %psum.63 = f32[]{:T(128)} all-reduce(f32[]{:T(128)} %multiply_reduce_fusion.5), channel_id=1, replica_groups=mesh['ray'=4,'vox'=8] {'ray','vox'}, use_global_device_ids=true, to_apply=%region_1.0 | all-reduce | flops 1 | bytes 8 | tf_op jit(solution)/shard_map/psum | solution.py:30
  51.4 0.7 compare_select_fusion
  52.7 0.9 fusion.19
  53.7 0.0 copy-start
  53.7 0.0 copy-start.1
  53.7 5.3 %fusion.26 = f32[64,1,128]{2,1,0:T(1,128)S(1)} fusion(f32[64,128,1]{1,2,0:T(1,128)S(1)} %bitcast.43, f32[64,128,128]{2,1,0:T(8,128)} %param.5), kind=kOutput, calls=%fused_computation.52 | convolution fusion | flops 12582912 | bytes 4259840 | tf_op jit(solution)/shard_map/tij,ti->tj/dot_general | solution.py:24
  59.0 1.5 scatter_custom_fusion
  60.5 0.0 reduce-scatter.4.cloned.1.call-update
  60.5 0.0 reduce-scatter.6.cloned.1.call-start
  60.6 61.7 %reduce-scatter.4.cloned.1.call-done = f32[64,128]{1,0:T(8,128)} async-done(((f32[512,128]{1,0:T(8,128)}), f32[64,128]{1,0:T(8,128)}) %reduce-scatter.4.cloned.1.call-update) | async-done | bytes 32784 | tf_op jit(solution)/shard_map/reduce_scatter | solution.py:26
  122.3 10.8 %psum.64 = f32[64,128]{1,0:T(8,128)S(1)} all-reduce(f32[64,128]{1,0:T(8,128)} %reduce-scatter.4.cloned.1.call-done), channel_id=1, replica_groups=mesh['ray'=4,'vox'=8] {'ray'}, use_global_device_ids=true, to_apply=%region_4.0 | all-reduce | flops 8192 | bytes 65536 | tf_op jit(solution)/shard_map/psum | solution.py:27
  133.1 0.6 multiply_reduce_fusion.2
  133.7 20.1 %psum.65 = f32[]{:T(128)} all-reduce(f32[]{:T(128)} %multiply_reduce_fusion.2), channel_id=1, replica_groups=mesh['ray'=4,'vox'=8] {'vox'}, use_global_device_ids=true, to_apply=%region_6.0 | all-reduce | flops 1 | bytes 8 | tf_op jit(solution)/shard_map/psum | solution.py:33
  154.5 30.9 %all_gather.6 = f32[512,128]{1,0:T(8,128)S(1)} all-gather(f32[64,128]{1,0:T(8,128)S(1)} %broadcast_divide_fusion.1), channel_id=1, replica_groups=mesh['ray'=4,'vox'=8] {'vox'}, dimensions={0}, use_global_device_ids=true | all-gather | bytes 294912 | tf_op jit(solution)/shard_map/all_gather | solution.py:45
  185.4 0.6 gather_fusion
  186.0 8.3 %fusion.27 = f32[64,1,128]{2,1,0:T(1,128)S(1)} fusion(f32[64,128,1]{1,2,0:T(1,128)S(1)} %bitcast.40, f32[64,128,128]{2,1,0:T(8,128)} %param.5), kind=kOutput, calls=%fused_computation.53 | convolution fusion | flops 12582912 | bytes 4259840 | tf_op jit(solution)/shard_map/tij,tj->ti/dot_general | solution.py:46
  194.3 0.0 copy-done
  194.3 0.0 copy-done.1
  194.3 0.8 multiply_reduce_fusion.4
  195.2 37.1 %psum.66 = f32[]{:T(128)} all-reduce(f32[]{:T(128)} %get-tuple-element.4), channel_id=1, replica_groups=mesh['ray'=4,'vox'=8] {'ray','vox'}, use_global_device_ids=true, to_apply=%region_8.0 | all-reduce | flops 1 | bytes 8 | tf_op jit(solution)/shard_map/psum | solution.py:30
  233.0 0.2 fusion.18
  233.2 5.3 %fusion.28 = f32[64,1,128]{2,1,0:T(1,128)S(1)} fusion(f32[64,128,1]{1,2,0:T(1,128)S(1)} %bitcast.44, f32[64,128,128]{2,1,0:T(8,128)} %param.5), kind=kOutput, calls=%fused_computation.54 | convolution fusion | flops 12582912 | bytes 4259840 | tf_op jit(solution)/shard_map/tij,ti->tj/dot_general | solution.py:24
  238.5 1.5 scatter_custom_fusion.1
  240.0 0.0 reduce-scatter.6.cloned.1.call-update
  240.0 0.0 reduce-scatter.8.cloned.1.call-start
  240.1 63.4 %reduce-scatter.6.cloned.1.call-done = f32[64,128]{1,0:T(8,128)} async-done(((f32[512,128]{1,0:T(8,128)}), f32[64,128]{1,0:T(8,128)}) %reduce-scatter.6.cloned.1.call-update) | async-done | bytes 32784 | tf_op jit(solution)/shard_map/reduce_scatter | solution.py:26
  303.4 10.8 %psum.67 = f32[64,128]{1,0:T(8,128)S(1)} all-reduce(f32[64,128]{1,0:T(8,128)} %reduce-scatter.6.cloned.1.call-done), channel_id=1, replica_groups=mesh['ray'=4,'vox'=8] {'ray'}, use_global_device_ids=true, to_apply=%region_11.0 | all-reduce | flops 8192 | bytes 65536 | tf_op jit(solution)/shard_map/psum | solution.py:27
  314.2 0.6 multiply_reduce_fusion.1
  314.9 20.1 %psum.68 = f32[]{:T(128)} all-reduce(f32[]{:T(128)} %multiply_reduce_fusion.1), channel_id=1, replica_groups=mesh['ray'=4,'vox'=8] {'vox'}, use_global_device_ids=true, to_apply=%region_13.0 | all-reduce | flops 1 | bytes 8 | tf_op jit(solution)/shard_map/psum | solution.py:33
  335.7 31.1 %all_gather.7 = f32[512,128]{1,0:T(8,128)S(1)} all-gather(f32[64,128]{1,0:T(8,128)S(1)} %broadcast_divide_fusion), channel_id=1, replica_groups=mesh['ray'=4,'vox'=8] {'vox'}, dimensions={0}, use_global_device_ids=true | all-gather | bytes 294912 | tf_op jit(solution)/shard_map/all_gather | solution.py:45
  366.7 0.6 gather_fusion.1
  367.3 8.3 %fusion.29 = f32[64,1,128]{2,1,0:T(1,128)S(1)} fusion(f32[64,128,1]{1,2,0:T(1,128)S(1)} %bitcast.38, f32[64,128,128]{2,1,0:T(8,128)} %param.5), kind=kOutput, calls=%fused_computation.55 | convolution fusion | flops 12582912 | bytes 4259840 | tf_op jit(solution)/shard_map/tij,tj->ti/dot_general | solution.py:46
  375.6 0.8 multiply_reduce_fusion.3
  376.4 37.1 %psum.69 = f32[]{:T(128)} all-reduce(f32[]{:T(128)} %get-tuple-element.6), channel_id=1, replica_groups=mesh['ray'=4,'vox'=8] {'ray','vox'}, use_global_device_ids=true, to_apply=%region_15.0 | all-reduce | flops 1 | bytes 8 | tf_op jit(solution)/shard_map/psum | solution.py:30
  414.3 0.2 fusion.16
  414.5 5.3 %fusion.30 = f32[64,1,128]{2,1,0:T(1,128)S(1)} fusion(f32[64,128,1]{1,2,0:T(1,128)S(1)} %bitcast.42, f32[64,128,128]{2,1,0:T(8,128)} %param.5), kind=kOutput, calls=%fused_computation.56 | convolution fusion | flops 12582912 | bytes 4259840 | tf_op jit(solution)/shard_map/tij,ti->tj/dot_general | solution.py:24
  419.8 1.5 scatter_custom_fusion.2
  421.3 0.0 reduce-scatter.8.cloned.1.call-update
  421.7 63.1 %reduce-scatter.8.cloned.1.call-done = f32[64,128]{1,0:T(8,128)} async-done(((f32[512,128]{1,0:T(8,128)}), f32[64,128]{1,0:T(8,128)}) %reduce-scatter.8.cloned.1.call-update) | async-done | bytes 32784 | tf_op jit(solution)/shard_map/reduce_scatter | solution.py:26
  484.8 10.8 %psum.70 = f32[64,128]{1,0:T(8,128)S(1)} all-reduce(f32[64,128]{1,0:T(8,128)} %reduce-scatter.8.cloned.1.call-done), channel_id=1, replica_groups=mesh['ray'=4,'vox'=8] {'ray'}, use_global_device_ids=true, to_apply=%region_18.0 | all-reduce | flops 8192 | bytes 65536 | tf_op jit(solution)/shard_map/psum | solution.py:27
  495.6 0.6 multiply_reduce_fusion
  496.2 20.1 %psum.71 = f32[]{:T(128)} all-reduce(f32[]{:T(128)} %multiply_reduce_fusion), channel_id=1, replica_groups=mesh['ray'=4,'vox'=8] {'vox'}, use_global_device_ids=true, to_apply=%region_20.0 | all-reduce | flops 1 | bytes 8 | tf_op jit(solution)/shard_map/psum | solution.py:33
  517.1 0.7 multiply_subtract_fusion
  (4 shorter events, 0.0 us)
Async XLA Ops:
  7.2 115.2 %reduce-scatter.4.cloned.1.call-start = ((), (), s32[]{:S(2)}) async-start(), calls=%async_computation.3 | async-start | bytes 294912 | tf_op jit(solution)/shard_map/reduce_scatter | solution.py:26
  53.7 140.7 %copy-start = (f32[16,128]{1,0:T(8,128)S(1)}, f32[16,128]{1,0:T(8,128)}, u32[]{:S(2)}) copy-start(f32[16,128]{1,0:T(8,128)} %param.9) | copy-start | bytes 24580
  53.7 140.7 %copy-start.1 = (s32[64]{0:T(128)S(1)}, s32[64]{0:T(128)}, u32[]{:S(2)}) copy-start(s32[64]{0:T(128)} %param.6) | copy-start | bytes 772
  60.5 242.9 %reduce-scatter.6.cloned.1.call-start = ((), (), s32[]{:S(2)}) async-start(), calls=%async_computation.4 | async-start | bytes 294912 | tf_op jit(solution)/shard_map/reduce_scatter | solution.py:26
  240.0 244.7 %reduce-scatter.8.cloned.1.call-start = ((), (), s32[]{:S(2)}) async-start(), calls=%async_computation.5 | async-start | bytes 294912 | tf_op jit(solution)/shard_map/reduce_scatter | solution.py:26
Sparse Core Ops, SparseCore 0:
  60.7 61.6 reduce-scatter.3
  240.2 63.2 reduce-scatter.5
  421.5 63.2 reduce-scatter.7
where the time goes:
time: 526 us; the launch traced here: 524 us
  blocking collectives  271 us (52%)
  waiting for transfers between devices  188 us (36%)
  matrix products  35.5 us (7%)
  between operations  19.1 us (4%)
  other arithmetic  9.11 us (2%)
    reduce_scatter x3, waiting for transfers between devices, backward(): lax.psum_scatter(partial_sum, 'vox', scatter_dimension=0, tiled=True)  188 us
    psum x3, blocking collectives, ray_length(): return jnp.sqrt(lax.psum(jnp.sum(ray_vec * ray_vec), ('ray', 'vox')))  116 us
    all_gather x2, blocking collectives, on_device(): whole = lax.all_gather(vox_vec, 'vox', axis=0, tiled=True)  62 us
    psum x3, blocking collectives, vox_length(): return jnp.sqrt(lax.psum(jnp.sum(vox_vec * vox_vec), 'vox'))  60.2 us
    psum x3, blocking collectives, backward(): return lax.psum(owned, 'ray')  32.4 us
    dot_general x2, matrix products, on_device(): jnp.einsum('tij,tj->ti', tiles, whole[tile_vox], precision=HIGH) * live  16.6 us
    dot_general x3, matrix products, backward(): prod = jnp.einsum('tij,ti->tj', tiles, rows_in, precision=HIGH) * live  15.8 us
  transfers between devices with their start and end apart: 3, of which 3 were waited for; matrix products, arithmetic and copies ran while one was open for 0% of the time, Pallas kernels for 0%

commit v1 on v0

--- a/solution.py
+++ b/solution.py
@@ -42,7 +42,15 @@
     phibar = beta_now
     rhobar = alpha_now
     for step in range(ITERS):
-        whole = lax.all_gather(vox_vec, "vox", axis=0, tiled=True)
+        ways, here, k = (lax.axis_size("vox"), lax.axis_index("vox"), vox_vec.shape[0])
+        line, have = (vox_vec, 1)
+        while have < ways:
+            line = jnp.concatenate(
+                [line, lax.ppermute(line, "vox", [(d, (d - have) % ways) for d in range(ways)])],
+                axis=0,
+            )
+            have = 2 * have
+        whole = jnp.roll(line, here * k, axis=0)
         forward_prod = jnp.einsum("tij,tj->ti", tiles, whole[tile_vox], precision=HIGH) * live
         ray_vec = jnp.dot(selector, forward_prod, precision=HIGH) - alpha_now * ray_vec
         beta_now = ray_length(ray_vec)

time: 526 us -> 498 us (0.947)
  blocking collectives: 271 us -> 213 us
  waiting for transfers between devices: 188 us -> 217 us
    all_gather x2 -> x0, blocking collectives: 62 us -> none  [on_device(): whole = lax.all_gather(vox_vec, 'vox', axis=0, tiled=True)]
    ppermute x0 -> x6, waiting for transfers between devices: none -> 31 us  [on_device(): lax.ppermute(line, 'vox', [(d, (d - have) % ways) for d in range(ways)])]
  transfers between devices with their start and end apart: 3 -> 9, of which waited for: 3 -> 9; matrix products, arithmetic and copies ran while one was open for 0% -> 0% of each run, Pallas kernels for 0% -> 0%
where the time goes in v1:
time: 498 us; the launch traced here: 496 us
  waiting for transfers between devices  217 us (44%)
  blocking collectives  213 us (43%)
  matrix products  35.5 us (7%)
  between operations  19.2 us (4%)
  other arithmetic  10.3 us (2%)
    reduce_scatter x3, waiting for transfers between devices, backward(): lax.psum_scatter(partial_sum, 'vox', scatter_dimension=0, tiled=True)  186 us
    psum x3, blocking collectives, ray_length(): return jnp.sqrt(lax.psum(jnp.sum(ray_vec * ray_vec), ('ray', 'vox')))  120 us
    psum x3, blocking collectives, vox_length(): return jnp.sqrt(lax.psum(jnp.sum(vox_vec * vox_vec), 'vox'))  60.3 us
    psum x3, blocking collectives, backward(): return lax.psum(owned, 'ray')  32.4 us
    ppermute x6, waiting for transfers between devices, on_device(): lax.ppermute(line, 'vox', [(d, (d - have) % ways) for d in range(ways)])  31 us
    dot_general x2, matrix products, on_device(): jnp.einsum('tij,tj->ti', tiles, whole[tile_vox], precision=HIGH) * live  16.6 us
    dot_general x3, matrix products, backward(): prod = jnp.einsum('tij,ti->tj', tiles, rows_in, precision=HIGH) * live  15.8 us
  transfers between devices with their start and end apart: 9, of which 9 were waited for; matrix products, arithmetic and copies ran while one was open for 0% of the time, Pallas kernels for 0%

profile of v1, /device:TPU:0, one launch (start us, length us, event | category | flops | bytes accessed | tf_op | source)
XLA Modules:
  0.0 496.3 jit_solution(4568662209399585600)
XLA Ops:
  7.2 0.0 reduce-scatter.4.cloned.1.call-start
  7.2 1.3 multiply_reduce_fusion.5
  8.5 42.2 %psum.63 = f32[]{:T(128)} all-reduce(f32[]{:T(128)} %multiply_reduce_fusion.5), channel_id=1, replica_groups=mesh['ray'=4,'vox'=8] {'ray','vox'}, use_global_device_ids=true, to_apply=%region_1.0 | all-reduce | flops 1 | bytes 8 | tf_op jit(solution)/shard_map/psum | solution.py:30
  51.4 0.7 compare_select_fusion
  52.7 0.9 fusion.33
  53.7 0.0 copy-start
  53.7 0.0 copy-start.1
  53.7 5.3 %fusion.40 = f32[64,1,128]{2,1,0:T(1,128)S(1)} fusion(f32[64,128,1]{1,2,0:T(1,128)S(1)} %bitcast.43, f32[64,128,128]{2,1,0:T(8,128)} %param.7), kind=kOutput, calls=%fused_computation.86 | convolution fusion | flops 12582912 | bytes 4259840 | tf_op jit(solution)/shard_map/tij,ti->tj/dot_general | solution.py:24
  59.0 1.5 scatter_custom_fusion
  60.5 0.0 reduce-scatter.4.cloned.1.call-update
  60.5 0.0 reduce-scatter.6.cloned.1.call-start
  60.6 61.7 %reduce-scatter.4.cloned.1.call-done = f32[64,128]{1,0:T(8,128)} async-done(((f32[512,128]{1,0:T(8,128)}), f32[64,128]{1,0:T(8,128)}) %reduce-scatter.4.cloned.1.call-update) | async-done | bytes 32784 | tf_op jit(solution)/shard_map/reduce_scatter | solution.py:26
  122.3 10.8 %psum.64 = f32[64,128]{1,0:T(8,128)S(1)} all-reduce(f32[64,128]{1,0:T(8,128)} %reduce-scatter.4.cloned.1.call-done), channel_id=1, replica_groups=mesh['ray'=4,'vox'=8] {'ray'}, use_global_device_ids=true, to_apply=%region_4.0 | all-reduce | flops 8192 | bytes 65536 | tf_op jit(solution)/shard_map/psum | solution.py:27
  133.1 0.6 multiply_reduce_fusion.2
  133.7 20.1 %psum.65 = f32[]{:T(128)} all-reduce(f32[]{:T(128)} %multiply_reduce_fusion.2), channel_id=1, replica_groups=mesh['ray'=4,'vox'=8] {'vox'}, use_global_device_ids=true, to_apply=%region_6.0 | all-reduce | flops 1 | bytes 8 | tf_op jit(solution)/shard_map/psum | solution.py:33
  154.5 0.1 collective-permute-start
  154.6 3.9 collective-permute-done
  158.5 0.0 collective-permute-start.1
  158.5 5.4 %collective-permute-done.1 = f32[128,128]{1,0:T(8,128)S(1)} collective-permute-done((f32[128,128]{1,0:T(8,128)S(1)}, f32[128,128]{1,0:T(8,128)S(1)}, u32[]{:S(2)}, u32[]{:S(2)}) %collective-permute-start.1) | collective-permute-done | bytes 65568 | tf_op jit(solution)/shard_map/ppermute | solution.py:49
  163.9 0.1 collective-permute-start.2
  164.0 6.2 %collective-permute-done.2 = f32[256,128]{1,0:T(8,128)S(1)} collective-permute-done((f32[256,128]{1,0:T(8,128)S(1)}, f32[256,128]{1,0:T(8,128)S(1)}, u32[]{:S(2)}, u32[]{:S(2)}) %collective-permute-start.2) | collective-permute-done | bytes 131104 | tf_op jit(solution)/shard_map/ppermute | solution.py:49
  170.2 0.6 fusion.10
  170.8 0.6 gather_fusion
  171.4 8.3 %fusion.41 = f32[64,1,128]{2,1,0:T(1,128)S(1)} fusion(f32[64,128,1]{1,2,0:T(1,128)S(1)} %bitcast.40, f32[64,128,128]{2,1,0:T(8,128)} %param.7), kind=kOutput, calls=%fused_computation.87 | convolution fusion | flops 12582912 | bytes 4259840 | tf_op jit(solution)/shard_map/tij,tj->ti/dot_general | solution.py:54
  179.7 0.0 copy-done
  179.7 0.0 copy-done.1
  179.7 0.8 multiply_reduce_fusion.4
  180.5 39.0 %psum.66 = f32[]{:T(128)} all-reduce(f32[]{:T(128)} %get-tuple-element.5), channel_id=1, replica_groups=mesh['ray'=4,'vox'=8] {'ray','vox'}, use_global_device_ids=true, to_apply=%region_8.10 | all-reduce | flops 1 | bytes 8 | tf_op jit(solution)/shard_map/psum | solution.py:30
  220.2 0.2 fusion.32
  220.4 5.3 %fusion.42 = f32[64,1,128]{2,1,0:T(1,128)S(1)} fusion(f32[64,128,1]{1,2,0:T(1,128)S(1)} %bitcast.44, f32[64,128,128]{2,1,0:T(8,128)} %param.7), kind=kOutput, calls=%fused_computation.88 | convolution fusion | flops 12582912 | bytes 4259840 | tf_op jit(solution)/shard_map/tij,ti->tj/dot_general | solution.py:24
  225.7 1.5 scatter_custom_fusion.1
  227.3 0.0 reduce-scatter.6.cloned.1.call-update
  227.3 0.0 reduce-scatter.8.cloned.1.call-start
  227.3 62.3 %reduce-scatter.6.cloned.1.call-done = f32[64,128]{1,0:T(8,128)} async-done(((f32[512,128]{1,0:T(8,128)}), f32[64,128]{1,0:T(8,128)}) %reduce-scatter.6.cloned.1.call-update) | async-done | bytes 32784 | tf_op jit(solution)/shard_map/reduce_scatter | solution.py:26
  289.6 10.8 %psum.67 = f32[64,128]{1,0:T(8,128)S(1)} all-reduce(f32[64,128]{1,0:T(8,128)} %reduce-scatter.6.cloned.1.call-done), channel_id=1, replica_groups=mesh['ray'=4,'vox'=8] {'ray'}, use_global_device_ids=true, to_apply=%region_11.13 | all-reduce | flops 8192 | bytes 65536 | tf_op jit(solution)/shard_map/psum | solution.py:27
  300.4 0.6 multiply_reduce_fusion.1
  301.0 20.1 %psum.68 = f32[]{:T(128)} all-reduce(f32[]{:T(128)} %multiply_reduce_fusion.1), channel_id=1, replica_groups=mesh['ray'=4,'vox'=8] {'vox'}, use_global_device_ids=true, to_apply=%region_13.15 | all-reduce | flops 1 | bytes 8 | tf_op jit(solution)/shard_map/psum | solution.py:33
  321.8 0.1 collective-permute-start.3
  321.9 3.9 collective-permute-done.3
  325.8 0.0 collective-permute-start.4
  325.8 5.3 %collective-permute-done.4 = f32[128,128]{1,0:T(8,128)S(1)} collective-permute-done((f32[128,128]{1,0:T(8,128)S(1)}, f32[128,128]{1,0:T(8,128)S(1)}, u32[]{:S(2)}, u32[]{:S(2)}) %collective-permute-start.4) | collective-permute-done | bytes 65568 | tf_op jit(solution)/shard_map/ppermute | solution.py:49
  331.2 0.1 collective-permute-start.5
  331.2 6.3 %collective-permute-done.5 = f32[256,128]{1,0:T(8,128)S(1)} collective-permute-done((f32[256,128]{1,0:T(8,128)S(1)}, f32[256,128]{1,0:T(8,128)S(1)}, u32[]{:S(2)}, u32[]{:S(2)}) %collective-permute-start.5) | collective-permute-done | bytes 131104 | tf_op jit(solution)/shard_map/ppermute | solution.py:49
  337.5 0.6 fusion.3
  338.1 0.6 gather_fusion.1
  338.7 8.3 %fusion.43 = f32[64,1,128]{2,1,0:T(1,128)S(1)} fusion(f32[64,128,1]{1,2,0:T(1,128)S(1)} %bitcast.38, f32[64,128,128]{2,1,0:T(8,128)} %param.7), kind=kOutput, calls=%fused_computation.89 | convolution fusion | flops 12582912 | bytes 4259840 | tf_op jit(solution)/shard_map/tij,tj->ti/dot_general | solution.py:54
  347.0 0.8 multiply_reduce_fusion.3
  347.8 39.0 %psum.69 = f32[]{:T(128)} all-reduce(f32[]{:T(128)} %get-tuple-element.7), channel_id=1, replica_groups=mesh['ray'=4,'vox'=8] {'ray','vox'}, use_global_device_ids=true, to_apply=%region_15.17 | all-reduce | flops 1 | bytes 8 | tf_op jit(solution)/shard_map/psum | solution.py:30
  387.5 0.2 fusion.30
  387.7 5.3 %fusion.44 = f32[64,1,128]{2,1,0:T(1,128)S(1)} fusion(f32[64,128,1]{1,2,0:T(1,128)S(1)} %bitcast.42, f32[64,128,128]{2,1,0:T(8,128)} %param.7), kind=kOutput, calls=%fused_computation.90 | convolution fusion | flops 12582912 | bytes 4259840 | tf_op jit(solution)/shard_map/tij,ti->tj/dot_general | solution.py:24
  393.0 1.5 scatter_custom_fusion.2
  394.5 0.0 reduce-scatter.8.cloned.1.call-update
  394.9 61.9 %reduce-scatter.8.cloned.1.call-done = f32[64,128]{1,0:T(8,128)} async-done(((f32[512,128]{1,0:T(8,128)}), f32[64,128]{1,0:T(8,128)}) %reduce-scatter.8.cloned.1.call-update) | async-done | bytes 32784 | tf_op jit(solution)/shard_map/reduce_scatter | solution.py:26
  456.8 10.8 %psum.70 = f32[64,128]{1,0:T(8,128)S(1)} all-reduce(f32[64,128]{1,0:T(8,128)} %reduce-scatter.8.cloned.1.call-done), channel_id=1, replica_groups=mesh['ray'=4,'vox'=8] {'ray'}, use_global_device_ids=true, to_apply=%region_18.20 | all-reduce | flops 8192 | bytes 65536 | tf_op jit(solution)/shard_map/psum | solution.py:27
  467.6 0.6 multiply_reduce_fusion
  468.3 20.1 %psum.71 = f32[]{:T(128)} all-reduce(f32[]{:T(128)} %multiply_reduce_fusion), channel_id=1, replica_groups=mesh['ray'=4,'vox'=8] {'vox'}, use_global_device_ids=true, to_apply=%region_20.22 | all-reduce | flops 1 | bytes 8 | tf_op jit(solution)/shard_map/psum | solution.py:33
  489.2 0.7 multiply_subtract_fusion
  (8 shorter events, 0.1 us)
Async XLA Ops:
  7.2 115.2 %reduce-scatter.4.cloned.1.call-start = ((), (), s32[]{:S(2)}) async-start(), calls=%async_computation.3 | async-start | bytes 294912 | tf_op jit(solution)/shard_map/reduce_scatter | solution.py:26
  53.7 126.0 %copy-start = (f32[16,128]{1,0:T(8,128)S(1)}, f32[16,128]{1,0:T(8,128)}, u32[]{:S(2)}) copy-start(f32[16,128]{1,0:T(8,128)} %param.11) | copy-start | bytes 24580
  53.7 126.0 %copy-start.1 = (s32[64]{0:T(128)S(1)}, s32[64]{0:T(128)}, u32[]{:S(2)}) copy-start(s32[64]{0:T(128)} %param.8) | copy-start | bytes 772
  60.5 229.0 %reduce-scatter.6.cloned.1.call-start = ((), (), s32[]{:S(2)}) async-start(), calls=%async_computation.4 | async-start | bytes 294912 | tf_op jit(solution)/shard_map/reduce_scatter | solution.py:26
  154.5 4.0 collective-permute-start
  158.5 5.4 %collective-permute-start.1 = (f32[128,128]{1,0:T(8,128)S(1)}, f32[128,128]{1,0:T(8,128)S(1)}, u32[]{:S(2)}, u32[]{:S(2)}) collective-permute-start(f32[128,128]{1,0:T(8,128)S(1)} %pad_maximum_fusion.2), channel_id=1, source_target_pairs={{0,6},{1,7},{2,0},{3,1},{4,2},{5,3},{6,4},{7,5},{8,14},{9,15},{10,... | collective-permute-start | bytes 196616 | tf_op jit(solution)/shard_map/ppermute | solution.py:49
  163.9 6.3 %collective-permute-start.2 = (f32[256,128]{1,0:T(8,128)S(1)}, f32[256,128]{1,0:T(8,128)S(1)}, u32[]{:S(2)}, u32[]{:S(2)}) collective-permute-start(f32[256,128]{1,0:T(8,128)S(1)} %pad_maximum_fusion), channel_id=1, source_target_pairs={{0,4},{1,5},{2,6},{3,7},{4,0},{5,1},{6,2},{7,3},{8,12},{9,13},{10,... | collective-permute-start | bytes 393224 | tf_op jit(solution)/shard_map/ppermute | solution.py:49
  227.3 229.6 %reduce-scatter.8.cloned.1.call-start = ((), (), s32[]{:S(2)}) async-start(), calls=%async_computation.5 | async-start | bytes 294912 | tf_op jit(solution)/shard_map/reduce_scatter | solution.py:26
  321.8 4.0 collective-permute-start.3
  325.8 5.3 %collective-permute-start.4 = (f32[128,128]{1,0:T(8,128)S(1)}, f32[128,128]{1,0:T(8,128)S(1)}, u32[]{:S(2)}, u32[]{:S(2)}) collective-permute-start(f32[128,128]{1,0:T(8,128)S(1)} %pad_maximum_fusion.3), channel_id=1, source_target_pairs={{0,6},{1,7},{2,0},{3,1},{4,2},{5,3},{6,4},{7,5},{8,14},{9,15},{10,... | collective-permute-start | bytes 196616 | tf_op jit(solution)/shard_map/ppermute | solution.py:49
  331.2 6.3 %collective-permute-start.5 = (f32[256,128]{1,0:T(8,128)S(1)}, f32[256,128]{1,0:T(8,128)S(1)}, u32[]{:S(2)}, u32[]{:S(2)}) collective-permute-start(f32[256,128]{1,0:T(8,128)S(1)} %pad_maximum_fusion.1), channel_id=1, source_target_pairs={{0,4},{1,5},{2,6},{3,7},{4,0},{5,1},{6,2},{7,3},{8,12},{9,13},{10,... | collective-permute-start | bytes 393224 | tf_op jit(solution)/shard_map/ppermute | solution.py:49
Sparse Core Ops, SparseCore 0:
  60.7 61.6 reduce-scatter.3
  227.4 62.1 reduce-scatter.5
  394.7 62.1 reduce-scatter.7
